TPU v7x, 32 devices: a whole 2x2x4 slice. The times are simulated.
32 devices in a mesh: strip: 8 (over y, x, core), mode: 4 (over z).
Axes of the slice: x: 2, y: 2, z: 4, core: 2. Of those that a mesh axis runs over, the one named last changes fastest.
Arguments:
- object_field: float32 [2, 2048, 384], P(None, 'strip'), may hold values from -5 to 5
- probe_modes: float32 [2, 8, 256, 256], P(None, 'mode'), may hold values from -2.5 to 2.5
- measured: float32 [8, 4, 256, 256], P('strip'), may hold values from 0.1 to 27
- positions: int32 [8, 4, 2], P('strip'), may hold values from 0 to 128, as said below
Outputs:
- object_new: float32 [2, 2048, 384], P(None, 'strip')
Inputs may be any that keep to these rules, and one draw needn't show every extreme that they name: positions[s,k,0] is the first row of window k within strip s and positions[s,k,1] its first column; the windows of every strip form a two by two raster with small offsets: windows 0 and 3 start at row 128, windows 1 and 2 at row 0, window 1 at column 128, window 3 at most 16 columns left of it, windows 0 and 2 at columns 0 to 16.
All inputs are finite; a program needn't handle non-finite values.
Results may differ from a plain program's by a relative error of at most 0.0001.
Values sent between devices are 32-bit elements; how exact they have to be, the bound alone decides.
A program may use at most 128 MiB of HBM per device.

v0:
```python
import jax
import jax.numpy as jnp
from jax import lax
from jax.sharding import PartitionSpec as P

HALO = 128
ITERS = 3
regularizer = 0.1
step_scale = 0.3
epsilon = 1e-06
highest = lax.Precision.HIGHEST


def from_behind(block, axis, distance):
    devices = range(lax.axis_size(axis))
    route = [(i - distance, i) for i in devices if i - distance in devices]
    return lax.ppermute(block, axis, route)


def dft_tables(length):
    indices = jnp.arange(length, dtype=jnp.int32)
    phases = indices[:, None] * indices[None, :] % length
    angles = phases.astype(jnp.float32) * (2.0 * jnp.pi / length)
    scaling = 1.0 / jnp.sqrt(jnp.float32(length))
    return (jnp.cos(angles) * scaling, -jnp.sin(angles) * scaling)


def transform(part_real, part_imag, cosine_table, sine_table):
    length = cosine_table.shape[0]
    stacked_rows = jnp.concatenate([cosine_table, sine_table], axis=0)
    left_real = jnp.einsum("jk,bkl->bjl", stacked_rows, part_real, precision=highest)
    left_imag = jnp.einsum("jk,bkl->bjl", stacked_rows, part_imag, precision=highest)
    middle_real = left_real[:, :length] - left_imag[:, length:]
    middle_imag = left_imag[:, :length] + left_real[:, length:]
    stacked_cols = jnp.concatenate([cosine_table, sine_table], axis=1)
    right_real = jnp.einsum("bjk,kl->bjl", middle_real, stacked_cols, precision=highest)
    right_imag = jnp.einsum("bjk,kl->bjl", middle_imag, stacked_cols, precision=highest)
    return (
        right_real[..., :length] - right_imag[..., length:],
        right_imag[..., :length] + right_real[..., length:],
    )


def body(object_field, probe_modes, measured, positions):
    stripe_rows = object_field.shape[1]
    width_cols = object_field.shape[2]
    window = probe_modes.shape[2]
    local_modes = probe_modes.shape[1]
    slots = positions.shape[1]
    halo_rows = HALO
    cosine_table, sine_table = dft_tables(window)
    rows_at = positions[0, :, 0]
    cols_at = positions[0, :, 1]
    total_cells = stripe_rows * lax.axis_size("strip") * width_cols
    measured_intensity = measured[0]
    probe_real = probe_modes[0][None]
    probe_imag = probe_modes[1][None]
    zero_index = jnp.zeros((), jnp.int32)
    for iteration in range(ITERS):
        below = from_behind(object_field[:, :halo_rows], "strip", -1)
        frame = jnp.concatenate([object_field, below], axis=1)
        patches = jnp.stack(
            [
                lax.dynamic_slice(
                    frame, (zero_index, rows_at[slot], cols_at[slot]), (2, window, window)
                )
                for slot in range(slots)
            ],
            axis=1,
        )
        patch_real = patches[0][:, None]
        patch_imag = patches[1][:, None]
        exit_real = probe_real * patch_real - probe_imag * patch_imag
        exit_imag = probe_real * patch_imag + probe_imag * patch_real
        far_real, far_imag = transform(
            exit_real.reshape(-1, window, window),
            exit_imag.reshape(-1, window, window),
            cosine_table,
            sine_table,
        )
        far_real = far_real.reshape(slots, local_modes, window, window)
        far_imag = far_imag.reshape(slots, local_modes, window, window)
        probe_power = jnp.sum(far_real * far_real + far_imag * far_imag, axis=1)
        summed_power = lax.psum(probe_power, "mode")
        object_update = (
            jnp.sqrt((measured_intensity + regularizer) / (summed_power + regularizer)) - 1.0
        )
        shift_real = (object_update[:, None] * far_real).reshape(-1, window, window)
        shift_imag = (object_update[:, None] * far_imag).reshape(-1, window, window)
        delta_real, delta_imag = transform(shift_real, shift_imag, cosine_table, -sine_table)
        delta_real = delta_real.reshape(slots, local_modes, window, window)
        delta_imag = delta_imag.reshape(slots, local_modes, window, window)
        grad_real = jnp.sum(probe_real * delta_real + probe_imag * delta_imag, axis=1)
        grad_imag = jnp.sum(probe_real * delta_imag - probe_imag * delta_real, axis=1)
        grad_real, grad_imag = lax.psum((grad_real, grad_imag), "mode")
        frame_grad = jnp.zeros((2, stripe_rows + halo_rows, width_cols), jnp.float32)
        for slot in range(slots):
            start = (zero_index, rows_at[slot], cols_at[slot])
            current = lax.dynamic_slice(frame_grad, start, (2, window, window))
            frame_grad = lax.dynamic_update_slice(
                frame_grad, current + jnp.stack([grad_real[slot], grad_imag[slot]]), start
            )
        arrived = from_behind(frame_grad[:, stripe_rows:], "strip", 1)
        gradient = jnp.concatenate(
            [frame_grad[:, :halo_rows] + arrived, frame_grad[:, halo_rows:stripe_rows]], axis=1
        )
        square_sum = lax.psum(jnp.sum(gradient * gradient), "strip")
        step_factor = step_scale / jnp.sqrt(square_sum / total_cells + epsilon)
        object_field = object_field + step_factor * gradient
    return object_field


def solution(mesh):
    return jax.shard_map(
        body,
        mesh=mesh,
        in_specs=(
            P(None, "strip", None),
            P(None, "mode", None, None),
            P("strip", None, None, None),
            P("strip", None, None),
        ),
        out_specs=P(None, "strip", None),
        check_vma=False,
    )
```

profile of v0, /device:TPU:4, one launch (start us, length us, event | category | flops | bytes accessed | tf_op | source)
XLA Modules:
  0.0 812.3 jit_solution(13496103538297187486)
XLA Ops:
  8.4 2.8 collective-permute-start
  31.6 7.1 convolution_bitcast_fusion.10
  38.7 7.5 convolution_bitcast_fusion.11
  46.3 3.7 fusion.22
  50.0 3.7 fusion.20
  53.7 1.9 copy-done.1
  58.5 51.5 %all-reduce.10.cloned.1.call-done = f32[4,256,256]{2,1,0:T(8,128)} async-done(((f32[4,256,256]{2,1,0:T(8,128)}), f32[4,256,256]{2,1,0:T(8,128)}) %all-reduce.10.cloned.1.call-update) | async-done | bytes 1048592 | tf_op jit(solution)/shard_map/psum | solution.py:84
  111.6 4.1 bitcast_multiply_fusion.5
  115.7 7.2 convolution_bitcast_fusion.9
  122.9 7.6 convolution_bitcast_fusion.8
  130.5 3.7 fusion.16
  134.2 3.7 fusion.18
  137.9 2.1 add_reduce_fusion.2
  140.1 85.5 %all-reduce.20.cloned.1.call-done = (f32[4,256,256]{2,1,0:T(8,128)}, f32[4,256,256]{2,1,0:T(8,128)}) async-done(((f32[4,256,256]{2,1,0:T(8,128)}, f32[4,256,256]{2,1,0:T(8,128)}), (f32[4,256,256]{2,1,0:T(8,128)}, f32[4,256,256]{2,1,0:T(8,128)})) %all-reduce.20.cloned.1.call-update) | async-done | bytes 2097168 | tf_op jit(solution)/shard_map/psum | solution.py:95
  225.6 2.2 fusion.109
  228.8 6.6 dynamic_update_slice.36
  236.6 5.3 dynamic_update_slice.37
  243.2 8.1 dynamic_update_slice.38
  252.5 6.6 dynamic_update_slice.39
  261.1 8.1 collective-permute-done.1
  270.8 12.5 %psum.87 = f32[]{:T(128)} all-reduce(f32[]{:T(128)} %multiply_reduce_fusion.2), channel_id=1, replica_groups=mesh['strip'=8,'mode'=4] {'strip'}, use_global_device_ids=true, to_apply=%region_7.8 | all-reduce | flops 1 | bytes 8 | tf_op jit(solution)/shard_map/psum | solution.py:107
  285.3 2.1 collective-permute-start.2
  287.4 5.1 collective-permute-done.2
  294.6 7.1 convolution_bitcast_fusion.6
  301.7 7.3 convolution_bitcast_fusion.7
  309.0 3.7 fusion.14
  312.8 3.7 fusion.12
  320.6 51.1 %all-reduce.12.cloned.1.call-done = f32[4,256,256]{2,1,0:T(8,128)} async-done(((f32[4,256,256]{2,1,0:T(8,128)}), f32[4,256,256]{2,1,0:T(8,128)}) %all-reduce.12.cloned.1.call-update) | async-done | bytes 1048592 | tf_op jit(solution)/shard_map/psum | solution.py:84
  373.3 4.1 bitcast_multiply_fusion.3
  377.4 7.2 convolution_bitcast_fusion.5
  384.6 7.4 convolution_bitcast_fusion.4
  391.9 3.7 fusion.8
  395.6 3.7 fusion.10
  399.3 2.1 add_reduce_fusion.1
  401.5 85.5 %all-reduce.18.cloned.1.call-done = (f32[4,256,256]{2,1,0:T(8,128)}, f32[4,256,256]{2,1,0:T(8,128)}) async-done(((f32[4,256,256]{2,1,0:T(8,128)}, f32[4,256,256]{2,1,0:T(8,128)}), (f32[4,256,256]{2,1,0:T(8,128)}, f32[4,256,256]{2,1,0:T(8,128)})) %all-reduce.18.cloned.1.call-update) | async-done | bytes 2097168 | tf_op jit(solution)/shard_map/psum | solution.py:95
  487.0 2.2 fusion.107
  490.2 6.6 dynamic_update_slice.40
  498.0 5.3 dynamic_update_slice.41
  504.6 8.1 dynamic_update_slice.42
  513.9 6.6 dynamic_update_slice.43
  522.5 8.1 collective-permute-done.3
  532.2 12.5 %psum.91 = f32[]{:T(128)} all-reduce(f32[]{:T(128)} %multiply_reduce_fusion.1), channel_id=1, replica_groups=mesh['strip'=8,'mode'=4] {'strip'}, use_global_device_ids=true, to_apply=%region_15.16 | all-reduce | flops 1 | bytes 8 | tf_op jit(solution)/shard_map/psum | solution.py:107
  546.8 2.3 collective-permute-start.4
  549.1 4.9 collective-permute-done.4
  556.1 7.1 convolution_bitcast_fusion.2
  563.1 7.2 convolution_bitcast_fusion.3
  570.4 3.7 fusion.6
  574.1 3.7 fusion.4
  581.7 51.3 %all-reduce.14.cloned.1.call-done = f32[4,256,256]{2,1,0:T(8,128)} async-done(((f32[4,256,256]{2,1,0:T(8,128)}), f32[4,256,256]{2,1,0:T(8,128)}) %all-reduce.14.cloned.1.call-update) | async-done | bytes 1048592 | tf_op jit(solution)/shard_map/psum | solution.py:84
  633.0 2.0 fusion.29
  634.9 4.1 bitcast_multiply_fusion.1
  639.0 7.2 convolution_bitcast_fusion.1
  646.2 7.6 convolution_bitcast_fusion
  653.8 3.7 fusion
  657.5 3.7 fusion.2
  661.2 2.1 add_reduce_fusion
  663.3 85.6 %all-reduce.16.cloned.1.call-done = (f32[4,256,256]{2,1,0:T(8,128)}, f32[4,256,256]{2,1,0:T(8,128)}) async-done(((f32[4,256,256]{2,1,0:T(8,128)}, f32[4,256,256]{2,1,0:T(8,128)}), (f32[4,256,256]{2,1,0:T(8,128)}, f32[4,256,256]{2,1,0:T(8,128)})) %all-reduce.16.cloned.1.call-update) | async-done | bytes 2097168 | tf_op jit(solution)/shard_map/psum | solution.py:95
  748.9 2.1 fusion.105
  751.9 6.8 dynamic_update_slice.44
  759.9 5.3 dynamic_update_slice.45
  765.4 8.1 dynamic_update_slice.46
  773.7 6.6 dynamic_update_slice.47
  782.2 8.1 collective-permute-done.5
  791.2 12.5 %psum.95 = f32[]{:T(128)} all-reduce(f32[]{:T(128)} %multiply_reduce_fusion), channel_id=1, replica_groups=mesh['strip'=8,'mode'=4] {'strip'}, use_global_device_ids=true, to_apply=%region_23.24 | all-reduce | flops 1 | bytes 8 | tf_op jit(solution)/shard_map/psum | solution.py:107
  (101 shorter events, 51.2 us)
Async XLA Ops:
  6.5 23.4 %copy-start.11 = (f32[2,2,256,256]{3,2,1,0:T(8,128)S(1)}, f32[2,2,256,256]{3,2,1,0:T(8,128)}, u32[]{:S(2)}) copy-start(f32[2,2,256,256]{3,2,1,0:T(8,128)} %param.5) | copy-start | bytes 3145732
  6.5 103.5 %all-reduce.10.cloned.1.call-start = ((), (), s32[]{:S(2)}) async-start(), calls=%async_computation | async-start | bytes 2097152 | tf_op jit(solution)/shard_map/psum | solution.py:84
  8.4 21.7 %collective-permute-start = (f32[2,128,384]{2,1,0:T(8,128)}, f32[2,128,384]{2,1,0:T(8,128)S(1)}, u32[]{:S(2)}, u32[]{:S(2)}) collective-permute-start(f32[2,128,384]{2,1,0:T(8,128)} %slice.359), channel_id=1, source_target_pairs={{4,0},{8,4},{12,8},{16,12},{20,16},{24,20},{28,24},{5,1},{9,5},{13... | collective-permute-start | bytes 1179656 | tf_op jit(solution)/shard_map/ppermute | solution.py:17
  50.0 3.7 copy-start
  53.7 1.9 copy-start.1
  55.7 54.3 %copy-start.7 = (f32[1,4,256,256]{3,2,1,0:T(8,128)S(1)}, f32[1,4,256,256]{3,2,1,0:T(8,128)}, u32[]{:S(2)}) copy-start(f32[1,4,256,256]{3,2,1,0:T(8,128)} %param.6) | copy-start | bytes 3145732
  57.4 168.2 %all-reduce.20.cloned.1.call-start = ((), (), s32[]{:S(2)}) async-start(), calls=%async_computation.5 | async-start | bytes 4194304 | tf_op jit(solution)/shard_map/psum | solution.py:95
  140.0 231.6 %all-reduce.12.cloned.1.call-start = ((), (), s32[]{:S(2)}) async-start(), calls=%async_computation.1 | async-start | bytes 2097152 | tf_op jit(solution)/shard_map/psum | solution.py:84
  225.6 2.2 copy-start.12
  259.1 10.0 %collective-permute-start.1 = (f32[2,128,384]{2,1,0:T(8,128)S(1)}, f32[2,128,384]{2,1,0:T(8,128)S(1)}, u32[]{:S(2)}, u32[]{:S(2)}) collective-permute-start(f32[2,128,384]{2,1,0:T(8,128)S(1)} %slice.485), channel_id=1, source_target_pairs={{0,4},{4,8},{8,12},{12,16},{16,20},{20,24},{24,28},{1,5},{5,9},{9,... | collective-permute-start | bytes 1179656 | tf_op jit(solution)/shard_map/ppermute | solution.py:17
  269.2 0.7 copy-start.10
  285.3 8.6 %copy-start.6 = (f32[2,256,384]{2,1,0:T(8,128)}, f32[2,256,384]{2,1,0:T(8,128)S(1)}, u32[]{:S(2)}) copy-start(f32[2,256,384]{2,1,0:T(8,128)S(1)} %multiply_add_fusion.8) | copy-start | bytes 2359300
  285.3 7.2 collective-permute-start.2
  312.7 3.7 copy-start.4
  316.5 1.9 copy-start.5
  318.4 53.2 %copy-start.8 = (f32[1,4,256,256]{3,2,1,0:T(8,128)S(1)}, f32[1,4,256,256]{3,2,1,0:T(8,128)}, u32[]{:S(2)}) copy-start(f32[1,4,256,256]{3,2,1,0:T(8,128)} %param.6) | copy-start | bytes 3145732
  320.0 167.0 %all-reduce.18.cloned.1.call-start = ((), (), s32[]{:S(2)}) async-start(), calls=%async_computation.4 | async-start | bytes 4194304 | tf_op jit(solution)/shard_map/psum | solution.py:95
  401.4 231.6 %all-reduce.14.cloned.1.call-start = ((), (), s32[]{:S(2)}) async-start(), calls=%async_computation.2 | async-start | bytes 2097152 | tf_op jit(solution)/shard_map/psum | solution.py:84
  487.0 2.2 copy-start.13
  520.5 10.0 %collective-permute-start.3 = (f32[2,128,384]{2,1,0:T(8,128)S(1)}, f32[2,128,384]{2,1,0:T(8,128)S(1)}, u32[]{:S(2)}, u32[]{:S(2)}) collective-permute-start(f32[2,128,384]{2,1,0:T(8,128)S(1)} %slice.515), channel_id=1, source_target_pairs={{0,4},{4,8},{8,12},{12,16},{16,20},{20,24},{24,28},{1,5},{5,9},{9,... | collective-permute-start | bytes 1179656 | tf_op jit(solution)/shard_map/ppermute | solution.py:17
  530.6 0.7 copy-start.9
  546.8 7.2 collective-permute-start.4
  574.1 3.7 copy-start.2
  577.8 1.9 copy-start.3
  581.4 167.5 %all-reduce.16.cloned.1.call-start = ((), (), s32[]{:S(2)}) async-start(), calls=%async_computation.3 | async-start | bytes 4194304 | tf_op jit(solution)/shard_map/psum | solution.py:95
  748.9 2.1 copy-start.14
  780.3 10.0 %collective-permute-start.5 = (f32[2,128,384]{2,1,0:T(8,128)S(1)}, f32[2,128,384]{2,1,0:T(8,128)S(1)}, u32[]{:S(2)}, u32[]{:S(2)}) collective-permute-start(f32[2,128,384]{2,1,0:T(8,128)S(1)} %slice.545), channel_id=1, source_target_pairs={{0,4},{4,8},{8,12},{12,16},{16,20},{20,24},{24,28},{1,5},{5,9},{9,... | collective-permute-start | bytes 1179656 | tf_op jit(solution)/shard_map/ppermute | solution.py:17
Sparse Core Ops, SparseCore 0:
  57.6 52.3 all-reduce.9
  140.1 85.4 all-reduce.19
  320.2 51.4 all-reduce.11
  401.5 85.4 all-reduce.17
  581.5 51.4 all-reduce.13
  663.4 85.4 all-reduce.15
where the time goes:
time: 822 us; the launch traced here: 812 us
  waiting for transfers between devices  445 us (54%)
  matrix products  132 us (16%)
  local copies, waits for them, and re-layouts  102 us (12%)
  other arithmetic  50.7 us (6%)
  blocking collectives  37.5 us (5%)
  between operations  31.3 us (4%)
  starting transfers between devices  13.8 us (2%)
    psum x3, waiting for transfers between devices, body(): grad_real, grad_imag = lax.psum((grad_real, grad_imag), 'mode')  257 us
    psum x3, waiting for transfers between devices, body(): summed_power = lax.psum(probe_power, 'mode')  154 us
    dynamic_update_slice x12, local copies, waits for them, and re-layouts, body(): lax.dynamic_update_slice(frame_grad, current + jnp.stack([grad_real[slot]...  79.7 us
    dot_general x6, matrix products, transform(): jnp.einsum('jk,bkl->bjl', stacked_rows, part_imag, precision=highest)  43.8 us
    dot_general x6, matrix products, transform(): jnp.einsum('jk,bkl->bjl', stacked_rows, part_real, precision=highest)  43.7 us
    psum x3, blocking collectives, body(): square_sum = lax.psum(jnp.sum(gradient * gradient), 'strip')  37.5 us
    ppermute x6, waiting for transfers between devices, from_behind(): return lax.ppermute(block, axis, route)  34.2 us
    dot_general x6, matrix products, transform(): jnp.einsum('bjk,kl->bjl', middle_real, stacked_cols, precision=highest)  22.2 us
  transfers between devices with their start and end apart: 12, of which 11 were waited for; matrix products, arithmetic and copies ran while one was open for 1% of the time, Pallas kernels for 0%

commit v1 on v0

--- a/solution.py
+++ b/solution.py
@@ -81,7 +81,11 @@
         far_real = far_real.reshape(slots, local_modes, window, window)
         far_imag = far_imag.reshape(slots, local_modes, window, window)
         probe_power = jnp.sum(far_real * far_real + far_imag * far_imag, axis=1)
-        summed_power = lax.psum(probe_power, "mode")
+        summed_power = probe_power
+        for hop in (1, 2):
+            summed_power = summed_power + lax.ppermute(
+                summed_power, "mode", [(dev, dev ^ hop) for dev in range(4)]
+            )
         object_update = (
             jnp.sqrt((measured_intensity + regularizer) / (summed_power + regularizer)) - 1.0
         )

time: 822 us -> 865 us (1.052)
  waiting for transfers between devices: 445 us -> 503 us
  other arithmetic: 50.7 us -> 35.9 us
    ppermute x0 -> x6, waiting for transfers between devices: none -> 211 us  [body(): lax.ppermute(summed_power, 'mode', [(dev, dev ^ hop) for dev in range(4)])]
    psum x3 -> x0, waiting for transfers between devices: 154 us -> none  [body(): summed_power = lax.psum(probe_power, 'mode')]
    mul x3, other arithmetic: 12.3 us -> 2 us  [body(): shift_real = (object_update[:, None] * far_real).reshape(-1, window, window)]
  transfers between devices with their start and end apart: 12 -> 15, of which waited for: 11 -> 14; matrix products, arithmetic and copies ran while one was open for 1% -> 1% of each run, Pallas kernels for 0% -> 0%
where the time goes in v1:
time: 865 us; the launch traced here: 856 us
  waiting for transfers between devices  503 us (58%)
  matrix products  131 us (15%)
  local copies, waits for them, and re-layouts  96.7 us (11%)
  blocking collectives  37.4 us (4%)
  other arithmetic  35.9 us (4%)
  between operations  30.7 us (4%)
  starting transfers between devices  20.9 us (2%)
    psum x3, waiting for transfers between devices, body(): grad_real, grad_imag = lax.psum((grad_real, grad_imag), 'mode')  257 us
    ppermute x6, waiting for transfers between devices, body(): lax.ppermute(summed_power, 'mode', [(dev, dev ^ hop) for dev in range(4)])  211 us
    dynamic_update_slice x12, local copies, waits for them, and re-layouts, body(): lax.dynamic_update_slice(frame_grad, current + jnp.stack([grad_real[slot]...  79.8 us
    dot_general x6, matrix products, transform(): jnp.einsum('jk,bkl->bjl', stacked_rows, part_imag, precision=highest)  43.4 us
    dot_general x6, matrix products, transform(): jnp.einsum('jk,bkl->bjl', stacked_rows, part_real, precision=highest)  42.5 us
    psum x3, blocking collectives, body(): square_sum = lax.psum(jnp.sum(gradient * gradient), 'strip')  37.4 us
    ppermute x6, waiting for transfers between devices, from_behind(): return lax.ppermute(block, axis, route)  34.6 us
    dot_general x6, matrix products, transform(): jnp.einsum('bjk,kl->bjl', middle_imag, stacked_cols, precision=highest)  22.6 us
  transfers between devices with their start and end apart: 15, of which 14 were waited for; matrix products, arithmetic and copies ran while one was open for 1% of the time, Pallas kernels for 0%

profile of v1, /device:TPU:4, one launch (start us, length us, event | category | flops | bytes accessed | tf_op | source)
XLA Modules:
  0.0 855.8 jit_solution(6176502635704196094)
XLA Ops:
  8.4 2.8 collective-permute-start
  31.4 7.0 convolution_bitcast_fusion.10
  38.3 6.9 convolution_bitcast_fusion.11
  45.2 3.8 fusion.22
  49.0 3.8 fusion.20
  55.4 23.1 %collective-permute-done.1 = f32[4,256,256]{2,1,0:T(8,128)S(1)} collective-permute-done((f32[4,256,256]{2,1,0:T(8,128)S(1)}, f32[4,256,256]{2,1,0:T(8,128)S(1)}, u32[]{:S(2)}, u32[]{:S(2)}) %collective-permute-start.1) | collective-permute-done | bytes 1048608 | tf_op jit(solution)/shard_map/ppermute | solution.py:86
  78.7 2.7 collective-permute-start.2
  82.3 43.6 %collective-permute-done.2 = f32[4,256,256]{2,1,0:T(8,128)S(1)} collective-permute-done((f32[4,256,256]{2,1,0:T(8,128)S(1)}, f32[4,256,256]{2,1,0:T(8,128)S(1)}, u32[]{:S(2)}, u32[]{:S(2)}) %collective-permute-start.2) | collective-permute-done | bytes 1048608 | tf_op jit(solution)/shard_map/ppermute | solution.py:86
  127.1 7.2 convolution_bitcast_fusion.9
  134.3 7.7 convolution_bitcast_fusion.8
  142.0 3.7 fusion.16
  145.7 3.7 fusion.18
  149.3 2.2 add_reduce_fusion.2
  151.7 88.2 %all-reduce.11.cloned.1.call-done = (f32[4,256,256]{2,1,0:T(8,128)}, f32[4,256,256]{2,1,0:T(8,128)}) async-done(((f32[4,256,256]{2,1,0:T(8,128)}, f32[4,256,256]{2,1,0:T(8,128)}), (f32[4,256,256]{2,1,0:T(8,128)}, f32[4,256,256]{2,1,0:T(8,128)})) %all-reduce.11.cloned.1.call-update) | async-done | bytes 2097168 | tf_op jit(solution)/shard_map/psum | solution.py:99
  239.9 2.2 fusion.109
  243.1 6.6 dynamic_update_slice.36
  251.0 5.3 dynamic_update_slice.37
  257.5 8.1 dynamic_update_slice.38
  266.8 6.6 dynamic_update_slice.39
  273.4 1.9 collective-permute-start.3
  275.4 8.1 collective-permute-done.3
  285.1 12.5 %psum.65 = f32[]{:T(128)} all-reduce(f32[]{:T(128)} %multiply_reduce_fusion.2), channel_id=1, replica_groups=mesh['strip'=8,'mode'=4] {'strip'}, use_global_device_ids=true, to_apply=%region_6.7 | all-reduce | flops 1 | bytes 8 | tf_op jit(solution)/shard_map/psum | solution.py:111
  299.6 1.9 collective-permute-start.4
  301.5 5.3 collective-permute-done.4
  309.0 7.0 convolution_bitcast_fusion.6
  316.0 7.1 convolution_bitcast_fusion.7
  323.1 3.8 fusion.14
  326.9 3.8 fusion.12
  331.9 24.9 %collective-permute-done.5 = f32[4,256,256]{2,1,0:T(8,128)S(1)} collective-permute-done((f32[4,256,256]{2,1,0:T(8,128)S(1)}, f32[4,256,256]{2,1,0:T(8,128)S(1)}, u32[]{:S(2)}, u32[]{:S(2)}) %collective-permute-start.5) | collective-permute-done | bytes 1048608 | tf_op jit(solution)/shard_map/ppermute | solution.py:86
  358.4 47.4 %collective-permute-done.6 = f32[4,256,256]{2,1,0:T(8,128)S(1)} collective-permute-done((f32[4,256,256]{2,1,0:T(8,128)S(1)}, f32[4,256,256]{2,1,0:T(8,128)S(1)}, u32[]{:S(2)}, u32[]{:S(2)}) %collective-permute-start.6) | collective-permute-done | bytes 1048608 | tf_op jit(solution)/shard_map/ppermute | solution.py:86
  407.1 7.2 convolution_bitcast_fusion.5
  414.3 7.6 convolution_bitcast_fusion.4
  421.9 3.7 fusion.8
  425.6 3.7 fusion.10
  429.3 2.1 add_reduce_fusion.1
  431.5 84.5 %all-reduce.9.cloned.1.call-done = (f32[4,256,256]{2,1,0:T(8,128)}, f32[4,256,256]{2,1,0:T(8,128)}) async-done(((f32[4,256,256]{2,1,0:T(8,128)}, f32[4,256,256]{2,1,0:T(8,128)}), (f32[4,256,256]{2,1,0:T(8,128)}, f32[4,256,256]{2,1,0:T(8,128)})) %all-reduce.9.cloned.1.call-update) | async-done | bytes 2097168 | tf_op jit(solution)/shard_map/psum | solution.py:99
  516.0 2.2 fusion.107
  519.2 6.6 dynamic_update_slice.40
  527.0 5.3 dynamic_update_slice.41
  533.6 8.1 dynamic_update_slice.42
  542.9 6.6 dynamic_update_slice.43
  551.4 8.1 collective-permute-done.7
  561.1 12.5 %psum.68 = f32[]{:T(128)} all-reduce(f32[]{:T(128)} %multiply_reduce_fusion.1), channel_id=1, replica_groups=mesh['strip'=8,'mode'=4] {'strip'}, use_global_device_ids=true, to_apply=%region_13.14 | all-reduce | flops 1 | bytes 8 | tf_op jit(solution)/shard_map/psum | solution.py:111
  575.6 2.1 collective-permute-start.8
  577.7 5.1 collective-permute-done.8
  584.9 7.0 convolution_bitcast_fusion.2
  591.9 6.9 convolution_bitcast_fusion.3
  598.8 3.8 fusion.6
  602.7 3.8 fusion.4
  607.6 24.9 %collective-permute-done.9 = f32[4,256,256]{2,1,0:T(8,128)S(1)} collective-permute-done((f32[4,256,256]{2,1,0:T(8,128)S(1)}, f32[4,256,256]{2,1,0:T(8,128)S(1)}, u32[]{:S(2)}, u32[]{:S(2)}) %collective-permute-start.9) | collective-permute-done | bytes 1048608 | tf_op jit(solution)/shard_map/ppermute | solution.py:86
  634.2 47.4 %collective-permute-done.10 = f32[4,256,256]{2,1,0:T(8,128)S(1)} collective-permute-done((f32[4,256,256]{2,1,0:T(8,128)S(1)}, f32[4,256,256]{2,1,0:T(8,128)S(1)}, u32[]{:S(2)}, u32[]{:S(2)}) %collective-permute-start.10) | collective-permute-done | bytes 1048608 | tf_op jit(solution)/shard_map/ppermute | solution.py:86
  683.1 7.2 convolution_bitcast_fusion.1
  690.3 7.2 convolution_bitcast_fusion
  697.5 3.7 fusion
  701.2 3.7 fusion.2
  704.9 2.1 add_reduce_fusion
  707.0 84.5 %all-reduce.7.cloned.1.call-done = (f32[4,256,256]{2,1,0:T(8,128)}, f32[4,256,256]{2,1,0:T(8,128)}) async-done(((f32[4,256,256]{2,1,0:T(8,128)}, f32[4,256,256]{2,1,0:T(8,128)}), (f32[4,256,256]{2,1,0:T(8,128)}, f32[4,256,256]{2,1,0:T(8,128)})) %all-reduce.7.cloned.1.call-update) | async-done | bytes 2097168 | tf_op jit(solution)/shard_map/psum | solution.py:99
  791.5 2.1 fusion.105
  794.6 6.8 dynamic_update_slice.44
  802.6 5.3 dynamic_update_slice.45
  809.1 8.1 dynamic_update_slice.46
  817.4 6.6 dynamic_update_slice.47
  826.0 8.1 collective-permute-done.11
  834.9 12.5 %psum.71 = f32[]{:T(128)} all-reduce(f32[]{:T(128)} %multiply_reduce_fusion), channel_id=1, replica_groups=mesh['strip'=8,'mode'=4] {'strip'}, use_global_device_ids=true, to_apply=%region_20.21 | all-reduce | flops 1 | bytes 8 | tf_op jit(solution)/shard_map/psum | solution.py:111
  (97 shorter events, 49.5 us)
Async XLA Ops:
  6.5 23.2 %copy-start.6 = (f32[2,2,256,256]{3,2,1,0:T(8,128)S(1)}, f32[2,2,256,256]{3,2,1,0:T(8,128)}, u32[]{:S(2)}) copy-start(f32[2,2,256,256]{3,2,1,0:T(8,128)} %param.5) | copy-start | bytes 3145732
  6.5 233.4 %all-reduce.11.cloned.1.call-start = ((), (), s32[]{:S(2)}) async-start(), calls=%async_computation.2 | async-start | bytes 4194304 | tf_op jit(solution)/shard_map/psum | solution.py:99
  8.4 21.4 %collective-permute-start = (f32[2,128,384]{2,1,0:T(8,128)}, f32[2,128,384]{2,1,0:T(8,128)S(1)}, u32[]{:S(2)}, u32[]{:S(2)}) collective-permute-start(f32[2,128,384]{2,1,0:T(8,128)} %slice.359), channel_id=1, source_target_pairs={{4,0},{8,4},{12,8},{16,12},{20,16},{24,20},{28,24},{5,1},{9,5},{13... | collective-permute-start | bytes 1179656 | tf_op jit(solution)/shard_map/ppermute | solution.py:17
  53.7 72.2 %copy-start.1 = (f32[1,4,256,256]{3,2,1,0:T(8,128)S(1)}, f32[1,4,256,256]{3,2,1,0:T(8,128)}, u32[]{:S(2)}) copy-start(f32[1,4,256,256]{3,2,1,0:T(8,128)} %param.6) | copy-start | bytes 3145732
  53.7 24.8 %collective-permute-start.1 = (f32[4,256,256]{2,1,0:T(8,128)S(1)}, f32[4,256,256]{2,1,0:T(8,128)S(1)}, u32[]{:S(2)}, u32[]{:S(2)}) collective-permute-start(f32[4,256,256]{2,1,0:T(8,128)S(1)} %bitcast_reduce_fusion.2), channel_id=1, source_target_pairs={{0,1},{1,0},{2,3},{3,2},{4,5},{5,4},{6,7},{7,6},{8,9},{9,8},{10,11... | collective-permute-start | bytes 3145736 | tf_op jit(solution)/shard_map/ppermute | solution.py:86
  78.7 47.3 %collective-permute-start.2 = (f32[4,256,256]{2,1,0:T(8,128)S(1)}, f32[4,256,256]{2,1,0:T(8,128)S(1)}, u32[]{:S(2)}, u32[]{:S(2)}) collective-permute-start(f32[4,256,256]{2,1,0:T(8,128)S(1)} %add.313), channel_id=1, source_target_pairs={{0,2},{1,3},{2,0},{3,1},{4,6},{5,7},{6,4},{7,5},{8,10},{9,11},{10,... | collective-permute-start | bytes 3145736 | tf_op jit(solution)/shard_map/ppermute | solution.py:86
  151.6 364.4 %all-reduce.9.cloned.1.call-start = ((), (), s32[]{:S(2)}) async-start(), calls=%async_computation.1 | async-start | bytes 4194304 | tf_op jit(solution)/shard_map/psum | solution.py:99
  239.9 2.2 copy-start.7
  273.4 10.0 %collective-permute-start.3 = (f32[2,128,384]{2,1,0:T(8,128)S(1)}, f32[2,128,384]{2,1,0:T(8,128)S(1)}, u32[]{:S(2)}, u32[]{:S(2)}) collective-permute-start(f32[2,128,384]{2,1,0:T(8,128)S(1)} %slice.485), channel_id=1, source_target_pairs={{0,4},{4,8},{8,12},{12,16},{16,20},{20,24},{24,28},{1,5},{5,9},{9,... | collective-permute-start | bytes 1179656 | tf_op jit(solution)/shard_map/ppermute | solution.py:17
  283.5 0.7 copy-start.5
  299.6 8.6 %copy-start = (f32[2,256,384]{2,1,0:T(8,128)}, f32[2,256,384]{2,1,0:T(8,128)S(1)}, u32[]{:S(2)}) copy-start(f32[2,256,384]{2,1,0:T(8,128)S(1)} %multiply_add_fusion.8) | copy-start | bytes 2359300
  299.6 7.2 collective-permute-start.4
  331.4 74.4 %copy-start.2 = (f32[1,4,256,256]{3,2,1,0:T(8,128)S(1)}, f32[1,4,256,256]{3,2,1,0:T(8,128)}, u32[]{:S(2)}) copy-start(f32[1,4,256,256]{3,2,1,0:T(8,128)} %param.6) | copy-start | bytes 3145732
  331.4 25.3 %collective-permute-start.5 = (f32[4,256,256]{2,1,0:T(8,128)S(1)}, f32[4,256,256]{2,1,0:T(8,128)S(1)}, u32[]{:S(2)}, u32[]{:S(2)}) collective-permute-start(f32[4,256,256]{2,1,0:T(8,128)S(1)} %bitcast_reduce_fusion.1), channel_id=1, source_target_pairs={{0,1},{1,0},{2,3},{3,2},{4,5},{5,4},{6,7},{7,6},{8,9},{9,8},{10,11... | collective-permute-start | bytes 3145736 | tf_op jit(solution)/shard_map/ppermute | solution.py:86
  356.9 48.9 %collective-permute-start.6 = (f32[4,256,256]{2,1,0:T(8,128)S(1)}, f32[4,256,256]{2,1,0:T(8,128)S(1)}, u32[]{:S(2)}, u32[]{:S(2)}) collective-permute-start(f32[4,256,256]{2,1,0:T(8,128)S(1)} %add.331), channel_id=1, source_target_pairs={{0,2},{1,3},{2,0},{3,1},{4,6},{5,7},{6,4},{7,5},{8,10},{9,11},{10,... | collective-permute-start | bytes 3145736 | tf_op jit(solution)/shard_map/ppermute | solution.py:86
  431.4 360.1 %all-reduce.7.cloned.1.call-start = ((), (), s32[]{:S(2)}) async-start(), calls=%async_computation | async-start | bytes 4194304 | tf_op jit(solution)/shard_map/psum | solution.py:99
  516.0 2.2 copy-start.8
  549.5 10.0 %collective-permute-start.7 = (f32[2,128,384]{2,1,0:T(8,128)S(1)}, f32[2,128,384]{2,1,0:T(8,128)S(1)}, u32[]{:S(2)}, u32[]{:S(2)}) collective-permute-start(f32[2,128,384]{2,1,0:T(8,128)S(1)} %slice.515), channel_id=1, source_target_pairs={{0,4},{4,8},{8,12},{12,16},{16,20},{20,24},{24,28},{1,5},{5,9},{9,... | collective-permute-start | bytes 1179656 | tf_op jit(solution)/shard_map/ppermute | solution.py:17
  559.6 0.7 copy-start.4
  575.6 7.2 collective-permute-start.8
  607.1 74.4 %copy-start.3 = (f32[1,4,256,256]{3,2,1,0:T(8,128)S(1)}, f32[1,4,256,256]{3,2,1,0:T(8,128)}, u32[]{:S(2)}) copy-start(f32[1,4,256,256]{3,2,1,0:T(8,128)} %param.6) | copy-start | bytes 3145732
  607.1 25.3 %collective-permute-start.9 = (f32[4,256,256]{2,1,0:T(8,128)S(1)}, f32[4,256,256]{2,1,0:T(8,128)S(1)}, u32[]{:S(2)}, u32[]{:S(2)}) collective-permute-start(f32[4,256,256]{2,1,0:T(8,128)S(1)} %bitcast_reduce_fusion), channel_id=1, source_target_pairs={{0,1},{1,0},{2,3},{3,2},{4,5},{5,4},{6,7},{7,6},{8,9},{9,8},{10,11... | collective-permute-start | bytes 3145736 | tf_op jit(solution)/shard_map/ppermute | solution.py:86
  632.6 48.9 %collective-permute-start.10 = (f32[4,256,256]{2,1,0:T(8,128)S(1)}, f32[4,256,256]{2,1,0:T(8,128)S(1)}, u32[]{:S(2)}, u32[]{:S(2)}) collective-permute-start(f32[4,256,256]{2,1,0:T(8,128)S(1)} %add.349), channel_id=1, source_target_pairs={{0,2},{1,3},{2,0},{3,1},{4,6},{5,7},{6,4},{7,5},{8,10},{9,11},{10,... | collective-permute-start | bytes 3145736 | tf_op jit(solution)/shard_map/ppermute | solution.py:86
  791.5 2.1 copy-start.9
  824.0 10.0 %collective-permute-start.11 = (f32[2,128,384]{2,1,0:T(8,128)S(1)}, f32[2,128,384]{2,1,0:T(8,128)S(1)}, u32[]{:S(2)}, u32[]{:S(2)}) collective-permute-start(f32[2,128,384]{2,1,0:T(8,128)S(1)} %slice.545), channel_id=1, source_target_pairs={{0,4},{4,8},{8,12},{12,16},{16,20},{20,24},{24,28},{1,5},{5,9},{9,... | collective-permute-start | bytes 1179656 | tf_op jit(solution)/shard_map/ppermute | solution.py:17
Sparse Core Ops, SparseCore 0:
  151.7 88.1 all-reduce.10
  431.5 84.3 all-reduce.8
  707.1 84.3 all-reduce.6
